TPU v7x, 512 devices: a whole 4x8x8 slice. The times are simulated.
512 devices in a mesh: tm: 32 (over y, z_lo), row: 16 (over x, z_hi, core).
Axes of the slice: x: 4, y: 8, z: 8 (z_hi: 2, z_lo: 4; z = z_hi * 4 + z_lo), core: 2. Of those that a mesh axis runs over, the one named last changes fastest.
Arguments:
- latents: bfloat16 [64, 96, 80, 256], P('tm', 'row'), may hold values from -6 to 6
- conv_weight: bfloat16 [3, 3, 768, 256], replicated, may hold values from -0.078125 to 0.078125
- norm_gain: float32 [256], replicated, may hold values from 0.1 to 1.9
- depth_target: bfloat16 [64, 96, 80, 128], P('tm', 'row'), may hold values from -6 to 6
Outputs:
- features: bfloat16 [64, 96, 80, 256], P('tm', 'row')
- gram: float32 [256, 256], replicated
- cross: float32 [256, 128], replicated
All inputs are finite; a program needn't handle non-finite values.
Results may differ from a plain program's by a relative error of at most 0.003.
Values may be sent and summed in bfloat16 or wider, within the bound.
A program may use at most 64 MiB of HBM per device.

v0:
```python
import jax
import jax.numpy as jnp
from jax import lax
from jax.sharding import PartitionSpec as P


def from_behind(value, axis, steps):
    count = lax.axis_size(axis)
    first, last = (max(0, -steps), min(count, count - steps))
    return lax.ppermute(value, axis, [(source, source + steps) for source in range(first, last)])


def extended(cells, sides, width):
    for axis, dim in sides:
        count = lax.axis_size(axis)
        ends = count - 1
        head = lax.slice_in_dim(cells, 0, width, axis=dim)
        tail = lax.slice_in_dim(cells, cells.shape[dim] - width, cells.shape[dim], axis=dim)
        cells = jnp.concatenate(
            [
                lax.ppermute(tail, axis, [(i, (i + 1) % count) for i in range(ends)]),
                cells,
                lax.ppermute(head, axis, [((i + 1) % count, i) for i in range(ends)]),
            ],
            axis=dim,
        )
    return cells


def convolve(padded, conv_weight):
    frames = padded.shape[0] - 2
    rows = padded.shape[1] - 2
    cols = padded.shape[2]
    chans = conv_weight.shape[3]
    wide = jnp.pad(padded, ((0, 0), (0, 0), (1, 1), (0, 0)))
    stacked = jnp.concatenate(
        [wide[:, :, 0:cols], wide[:, :, 1 : cols + 1], wide[:, :, 2 : cols + 2]], axis=3
    )
    total = jnp.zeros((frames * rows * cols, chans), jnp.float32)
    for dtime in range(3):
        for drow in range(3):
            piece = stacked[dtime : dtime + frames, drow : drow + rows].reshape(
                frames * rows * cols, -1
            )
            total = total + jnp.dot(
                piece, conv_weight[dtime, drow], preferred_element_type=jnp.float32
            )
    return total


def on_device(latents, conv_weight, norm_gain, depth_target):
    cached = from_behind(latents, "tm", 1)
    joined = jnp.concatenate([cached, latents], axis=0)
    padded = extended(joined, (("row", 1),), 1)
    conv = convolve(padded, conv_weight)
    flat_in = latents.reshape(conv.shape[0], conv.shape[1]).astype(jnp.float32)
    normed = conv * jax.lax.rsqrt(jnp.mean(conv * conv, axis=1, keepdims=True) + 1e-06) * norm_gain
    flat = (flat_in + jax.nn.silu(normed)).astype(jnp.bfloat16)
    targets = depth_target.reshape(flat.shape[0], -1)
    gram_part = jnp.dot(flat.T, flat, preferred_element_type=jnp.float32)
    cross_part = jnp.dot(flat.T, targets, preferred_element_type=jnp.float32)
    count = flat.shape[0] * lax.axis_size("tm") * lax.axis_size("row")
    gram_sum, cross_sum = lax.psum((gram_part, cross_part), ("tm", "row"))
    return (flat.reshape(latents.shape), gram_sum / count, cross_sum / count)


def solution(mesh):
    in_specs = (P("tm", "row", None, None), P(), P(), P("tm", "row", None, None))
    out_specs = (P("tm", "row", None, None), P(), P())
    return jax.shard_map(
        on_device, mesh=mesh, in_specs=in_specs, out_specs=out_specs, check_vma=False
    )
```

profile of v0, /device:TPU:1, one launch (start us, length us, event | category | flops | bytes accessed | tf_op | source)
XLA Modules:
  0.0 338.9 jit_solution(941491397047165075)
XLA Ops:
  7.2 0.0 copy-start
  7.2 0.0 all-reduce.4.cloned.1.call-start
  7.2 5.0 %collective-permute-start = (bf16[2,6,80,256]{3,2,1,0:T(8,128)(2,1)}, bf16[2,6,80,256]{3,2,1,0:T(8,128)(2,1)S(1)}, u32[]{:S(2)}, u32[]{:S(2)}) collective-permute-start(bf16[2,6,80,256]{3,2,1,0:T(8,128)(2,1)} %param.4), channel_id=1, source_target_pairs={{0,16},{16,32},{32,48},{48,64},{64,80},{80,96},{96,112},{112,128},... | collective-permute-start | bytes 1474568 | tf_op jit(solution)/shard_map/ppermute | solution.py:10
  12.2 7.8 %collective-permute-done = bf16[2,6,80,256]{3,2,1,0:T(8,128)(2,1)S(1)} collective-permute-done((bf16[2,6,80,256]{3,2,1,0:T(8,128)(2,1)}, bf16[2,6,80,256]{3,2,1,0:T(8,128)(2,1)S(1)}, u32[]{:S(2)}, u32[]{:S(2)}) %collective-permute-start) | collective-permute-done | bytes 491552 | tf_op jit(solution)/shard_map/ppermute | solution.py:10
  20.1 1.1 constant_dynamic-update-slice_fusion
  21.2 13.5 %collective-permute-start.1 = (bf16[4,1,80,256]{3,2,1,0:T(8,128)(2,1)S(1)}, bf16[4,1,80,256]{3,2,1,0:T(8,128)(2,1)S(1)}, u32[]{:S(2)}, u32[]{:S(2)}) collective-permute-start(bf16[4,1,80,256]{3,2,1,0:T(8,128)(2,1)S(1)} %get-tuple-element.16), channel_id=1, source_target_pairs={{0,1},{1,2},{2,3},{3,4},{4,5},{5,6},{6,7},{7,8},{8,9},{9,10},{10,1... | collective-permute-start | bytes 491528 | tf_op jit(solution)/shard_map/ppermute | solution.py:21
  34.7 1.9 collective-permute-start.2
  36.6 2.1 collective-permute-done.1
  38.7 7.3 %collective-permute-done.2 = bf16[4,1,80,256]{3,2,1,0:T(8,128)(2,1)S(1)} collective-permute-done((bf16[4,1,80,256]{3,2,1,0:T(8,128)(2,1)S(1)}, bf16[4,1,80,256]{3,2,1,0:T(8,128)(2,1)S(1)}, u32[]{:S(2)}, u32[]{:S(2)}) %collective-permute-start.2) | collective-permute-done | bytes 163872 | tf_op jit(solution)/shard_map/ppermute | solution.py:23
  46.0 0.8 fusion.5
  46.7 0.9 fusion.41
  47.6 0.3 pad_maximum_fusion
  48.0 0.0 copy-start.1
  48.0 1.2 fusion.40
  49.2 0.7 copy-done.1
  50.0 0.5 fusion.14
  50.5 0.5 fusion.16
  51.1 0.5 fusion.18
  51.6 0.5 fusion.20
  52.2 0.5 fusion.22
  52.8 0.5 fusion.24
  53.3 0.5 fusion.26
  53.9 0.5 fusion.28
  54.4 0.0 copy-start.2
  54.4 0.0 copy-start.4
  54.5 0.9 multiply_reduce_fusion
  55.4 0.1 copy-done.2
  55.5 0.0 copy-done.4
  55.5 0.4 fusion.13
  55.9 0.0 copy-start.3
  55.9 1.1 fusion.43
  56.9 0.0 copy-done
  56.9 1.0 fusion.44
  57.9 0.0 all-reduce.4.cloned.1.call-update
  58.0 270.9 %all-reduce.4.cloned.1.call-done = (f32[256,256]{1,0:T(8,128)}, f32[256,128]{1,0:T(8,128)}) async-done(((f32[256,256]{1,0:T(8,128)}, f32[256,128]{1,0:T(8,128)}), (f32[256,256]{1,0:T(8,128)}, f32[256,128]{1,0:T(8,128)})) %all-reduce.4.cloned.1.call-update) | async-done | bytes 393232 | tf_op jit(solution)/shard_map/psum | solution.py:63
  328.8 1.7 broadcast_multiply_fusion
  330.5 0.0 copy-done.3
  330.5 1.6 broadcast_multiply_fusion.1
  (3 shorter events, 0.1 us)
Async XLA Ops:
  7.2 49.8 %copy-start = (bf16[2,6,80,128]{3,2,1,0:T(8,128)(2,1)S(1)}, bf16[2,6,80,128]{3,2,1,0:T(8,128)(2,1)}, u32[]{:S(2)}) copy-start(bf16[2,6,80,128]{3,2,1,0:T(8,128)(2,1)} %param.7) | copy-start | bytes 737284
  7.2 321.6 %all-reduce.4.cloned.1.call-start = ((), (), s32[]{:S(2)}) async-start(), calls=%async_computation | async-start | bytes 786432 | tf_op jit(solution)/shard_map/psum | solution.py:63
  7.2 12.8 %collective-permute-start = (bf16[2,6,80,256]{3,2,1,0:T(8,128)(2,1)}, bf16[2,6,80,256]{3,2,1,0:T(8,128)(2,1)S(1)}, u32[]{:S(2)}, u32[]{:S(2)}) collective-permute-start(bf16[2,6,80,256]{3,2,1,0:T(8,128)(2,1)} %param.4), channel_id=1, source_target_pairs={{0,16},{16,32},{32,48},{48,64},{64,80},{80,96},{96,112},{112,128},... | collective-permute-start | bytes 1474568 | tf_op jit(solution)/shard_map/ppermute | solution.py:10
  21.2 17.5 %collective-permute-start.1 = (bf16[4,1,80,256]{3,2,1,0:T(8,128)(2,1)S(1)}, bf16[4,1,80,256]{3,2,1,0:T(8,128)(2,1)S(1)}, u32[]{:S(2)}, u32[]{:S(2)}) collective-permute-start(bf16[4,1,80,256]{3,2,1,0:T(8,128)(2,1)S(1)} %get-tuple-element.16), channel_id=1, source_target_pairs={{0,1},{1,2},{2,3},{3,4},{4,5},{5,6},{6,7},{7,8},{8,9},{9,10},{10,1... | collective-permute-start | bytes 491528 | tf_op jit(solution)/shard_map/ppermute | solution.py:21
  34.7 11.3 %collective-permute-start.2 = (bf16[4,1,80,256]{3,2,1,0:T(8,128)(2,1)S(1)}, bf16[4,1,80,256]{3,2,1,0:T(8,128)(2,1)S(1)}, u32[]{:S(2)}, u32[]{:S(2)}) collective-permute-start(bf16[4,1,80,256]{3,2,1,0:T(8,128)(2,1)S(1)} %get-tuple-element.17), channel_id=1, source_target_pairs={{1,0},{2,1},{3,2},{4,3},{5,4},{6,5},{7,6},{8,7},{9,8},{10,9},{11,1... | collective-permute-start | bytes 491528 | tf_op jit(solution)/shard_map/ppermute | solution.py:23
  48.0 2.0 copy-start.1
  54.4 1.0 copy-start.2
  54.4 1.0 copy-start.4
  55.9 274.6 %copy-start.3 = (bf16[960,256]{1,0:T(8,128)(2,1)}, bf16[960,256]{1,0:T(8,128)(2,1)S(1)}, u32[]{:S(2)}) copy-start(bf16[960,256]{1,0:T(8,128)(2,1)S(1)} %fusion.13) | copy-start | bytes 1474564
Sparse Core Ops, SparseCore 0:
  58.1 270.6 all-reduce.3
where the time goes:
time: 339 us
  waiting for transfers between devices  288 us (85%)
  starting transfers between devices  20.4 us (6%)
  between operations  14.2 us (4%)
  matrix products  7.34 us (2%)
  other arithmetic  4.74 us (1%)
  local copies, waits for them, and re-layouts  4.12 us (1%)
    psum x1, waiting for transfers between devices, on_device(): gram_sum, cross_sum = lax.psum((gram_part, cross_part), ('tm', 'row'))  271 us
    ppermute x1, starting transfers between devices, extended(): lax.ppermute(tail, axis, [(i, (i + 1) % count) for i in range(ends)])  13.5 us
    ppermute x1, waiting for transfers between devices, from_behind(): lax.ppermute(value, axis, [(source, source + steps) for source in range(f...  7.81 us
    ppermute x1, waiting for transfers between devices, extended(): lax.ppermute(head, axis, [((i + 1) % count, i) for i in range(ends)])  7.3 us
  transfers between devices with their start and end apart: 4, of which 4 were waited for; matrix products, arithmetic and copies ran while one was open for 0% of the time, Pallas kernels for 0%

commit v1 on v0

--- a/solution.py
+++ b/solution.py
@@ -2,6 +2,11 @@
 import jax.numpy as jnp
 from jax import lax
 from jax.sharding import PartitionSpec as P
+from jax.lax import psum
+
+expand_the_tails = lambda mine, group_axis, ax_name: psum(
+    psum(mine, axis_name=group_axis), axis_name=ax_name
+)
 
 
 def from_behind(value, axis, steps):
@@ -60,7 +65,7 @@
     gram_part = jnp.dot(flat.T, flat, preferred_element_type=jnp.float32)
     cross_part = jnp.dot(flat.T, targets, preferred_element_type=jnp.float32)
     count = flat.shape[0] * lax.axis_size("tm") * lax.axis_size("row")
-    gram_sum, cross_sum = lax.psum((gram_part, cross_part), ("tm", "row"))
+    gram_sum, cross_sum = expand_the_tails((gram_part, cross_part), "row", "tm")
     return (flat.reshape(latents.shape), gram_sum / count, cross_sum / count)
 
 

time: 339 us -> 556 us (1.64)
  the two profiles are of different devices: /device:TPU:1 before, /device:TPU:2 now
where the time goes in v1:
time: 556 us
  waiting for transfers between devices  510 us (92%)
  starting transfers between devices  15 us (3%)
  between operations  14.2 us (3%)
  matrix products  7.34 us (1%)
    psum x1, waiting for transfers between devices, psum(psum(mine, axis_name=group_axis), axis_name=ax_name)  313 us
    psum x1, waiting for transfers between devices, psum(mine, axis_name=group_axis)  181 us
  transfers between devices with their start and end apart: 5, of which 5 were waited for; matrix products, arithmetic and copies ran while one was open for 0% of the time, Pallas kernels for 0%

profile of v1, /device:TPU:2, one launch (start us, length us, event | category | flops | bytes accessed | tf_op | source)
XLA Modules:
  0.0 555.6 jit_solution(13335660412421570100)
XLA Ops:
  7.2 0.0 copy-start
  7.2 0.0 all-reduce.8.cloned.1.call-start
  7.2 4.4 collective-permute-start
  11.7 10.7 %collective-permute-done = bf16[2,6,80,256]{3,2,1,0:T(8,128)(2,1)S(1)} collective-permute-done((bf16[2,6,80,256]{3,2,1,0:T(8,128)(2,1)}, bf16[2,6,80,256]{3,2,1,0:T(8,128)(2,1)S(1)}, u32[]{:S(2)}, u32[]{:S(2)}) %collective-permute-start) | collective-permute-done | bytes 491552 | tf_op jit(solution)/shard_map/ppermute | solution.py:15
  22.5 1.1 constant_dynamic-update-slice_fusion
  23.6 1.9 collective-permute-start.1
  25.5 8.6 %collective-permute-start.2 = (bf16[4,1,80,256]{3,2,1,0:T(8,128)(2,1)S(1)}, bf16[4,1,80,256]{3,2,1,0:T(8,128)(2,1)S(1)}, u32[]{:S(2)}, u32[]{:S(2)}) collective-permute-start(bf16[4,1,80,256]{3,2,1,0:T(8,128)(2,1)S(1)} %get-tuple-element.19), channel_id=1, source_target_pairs={{1,0},{2,1},{3,2},{4,3},{5,4},{6,5},{7,6},{8,7},{9,8},{10,9},{11,1... | collective-permute-start | bytes 491528 | tf_op jit(solution)/shard_map/ppermute | solution.py:28
  34.1 1.1 collective-permute-done.1
  35.1 4.2 collective-permute-done.2
  39.3 0.8 fusion.5
  40.1 0.9 fusion.41
  41.0 0.3 pad_maximum_fusion
  41.3 0.0 copy-start.1
  41.3 1.2 fusion.40
  42.6 0.7 copy-done.1
  43.3 0.5 fusion.14
  43.9 0.5 fusion.16
  44.4 0.5 fusion.18
  45.0 0.5 fusion.20
  45.6 0.5 fusion.22
  46.1 0.5 fusion.24
  46.7 0.5 fusion.26
  47.2 0.5 fusion.28
  47.8 0.0 copy-start.2
  47.8 0.0 copy-start.4
  47.8 0.9 multiply_reduce_fusion
  48.7 0.1 copy-done.2
  48.8 0.0 copy-done.4
  48.8 0.4 fusion.13
  49.2 0.0 copy-start.3
  49.2 1.0 fusion.43
  50.3 0.0 copy-done
  50.3 1.0 fusion.44
  51.3 0.0 all-reduce.8.cloned.1.call-update
  51.3 0.0 all-reduce.6.cloned.1.call-start
  51.4 181.0 %all-reduce.8.cloned.1.call-done = (f32[256,256]{1,0:T(8,128)}, f32[256,128]{1,0:T(8,128)}) async-done(((f32[256,256]{1,0:T(8,128)}, f32[256,128]{1,0:T(8,128)}), (f32[256,256]{1,0:T(8,128)}, f32[256,128]{1,0:T(8,128)})) %all-reduce.8.cloned.1.call-update) | async-done | bytes 393232 | tf_op jit(solution)/shard_map/psum | solution.py:8
  232.4 0.0 all-reduce.6.cloned.1.call-update
  232.4 313.1 %all-reduce.6.cloned.1.call-done = (f32[256,256]{1,0:T(8,128)}, f32[256,128]{1,0:T(8,128)}) async-done(((f32[256,256]{1,0:T(8,128)}, f32[256,128]{1,0:T(8,128)}), (f32[256,256]{1,0:T(8,128)}, f32[256,128]{1,0:T(8,128)})) %all-reduce.6.cloned.1.call-update) | async-done | bytes 393232 | tf_op jit(solution)/shard_map/psum | solution.py:7
  545.5 1.7 broadcast_multiply_fusion
  547.2 0.0 copy-done.3
  547.2 1.6 broadcast_multiply_fusion.1
  (3 shorter events, 0.1 us)
Async XLA Ops:
  7.2 43.1 %copy-start = (bf16[2,6,80,128]{3,2,1,0:T(8,128)(2,1)S(1)}, bf16[2,6,80,128]{3,2,1,0:T(8,128)(2,1)}, u32[]{:S(2)}) copy-start(bf16[2,6,80,128]{3,2,1,0:T(8,128)(2,1)} %param.7) | copy-start | bytes 737284
  7.2 225.2 %all-reduce.8.cloned.1.call-start = ((), (), s32[]{:S(2)}) async-start(), calls=%async_computation.1 | async-start | bytes 786432 | tf_op jit(solution)/shard_map/psum | solution.py:8
  7.2 15.2 %collective-permute-start = (bf16[2,6,80,256]{3,2,1,0:T(8,128)(2,1)}, bf16[2,6,80,256]{3,2,1,0:T(8,128)(2,1)S(1)}, u32[]{:S(2)}, u32[]{:S(2)}) collective-permute-start(bf16[2,6,80,256]{3,2,1,0:T(8,128)(2,1)} %param.4), channel_id=1, source_target_pairs={{0,16},{16,32},{32,48},{48,64},{64,80},{80,96},{96,112},{112,128},... | collective-permute-start | bytes 1474568 | tf_op jit(solution)/shard_map/ppermute | solution.py:15
  23.6 11.6 %collective-permute-start.1 = (bf16[4,1,80,256]{3,2,1,0:T(8,128)(2,1)S(1)}, bf16[4,1,80,256]{3,2,1,0:T(8,128)(2,1)S(1)}, u32[]{:S(2)}, u32[]{:S(2)}) collective-permute-start(bf16[4,1,80,256]{3,2,1,0:T(8,128)(2,1)S(1)} %get-tuple-element.18), channel_id=1, source_target_pairs={{0,1},{1,2},{2,3},{3,4},{4,5},{5,6},{6,7},{7,8},{8,9},{9,10},{10,1... | collective-permute-start | bytes 491528 | tf_op jit(solution)/shard_map/ppermute | solution.py:26
  25.5 13.8 %collective-permute-start.2 = (bf16[4,1,80,256]{3,2,1,0:T(8,128)(2,1)S(1)}, bf16[4,1,80,256]{3,2,1,0:T(8,128)(2,1)S(1)}, u32[]{:S(2)}, u32[]{:S(2)}) collective-permute-start(bf16[4,1,80,256]{3,2,1,0:T(8,128)(2,1)S(1)} %get-tuple-element.19), channel_id=1, source_target_pairs={{1,0},{2,1},{3,2},{4,3},{5,4},{6,5},{7,6},{8,7},{9,8},{10,9},{11,1... | collective-permute-start | bytes 491528 | tf_op jit(solution)/shard_map/ppermute | solution.py:28
  41.3 2.0 copy-start.1
  47.8 1.0 copy-start.2
  47.8 1.0 copy-start.4
  49.2 498.0 %copy-start.3 = (bf16[960,256]{1,0:T(8,128)(2,1)}, bf16[960,256]{1,0:T(8,128)(2,1)S(1)}, u32[]{:S(2)}) copy-start(bf16[960,256]{1,0:T(8,128)(2,1)S(1)} %fusion.13) | copy-start | bytes 1474564
  51.3 494.2 %all-reduce.6.cloned.1.call-start = ((), (), s32[]{:S(2)}) async-start(), calls=%async_computation | async-start | bytes 786432 | tf_op jit(solution)/shard_map/psum | solution.py:7
Sparse Core Ops, SparseCore 0:
  51.4 180.9 all-reduce.7
  235.4 310.0 all-reduce.5
